TPU v7x, 256 devices: a whole 4x4x8 slice. The times are simulated.
256 devices in a mesh: dp: 2 (over y_lo), fsdp: 16 (over z, core), ctx: 8 (over x, y_hi).
Axes of the slice: x: 4, y: 4 (y_hi: 2, y_lo: 2; y = y_hi * 2 + y_lo), z: 8, core: 2. Of those that a mesh axis runs over, the one named last changes fastest.
Arguments:
- inputs: bfloat16 [32, 1024, 16384], P(('dp', 'fsdp'), 'ctx'), may hold values from -14.5 to 14.5
- cotangent: bfloat16 [32, 1024, 2048], P(('dp', 'fsdp'), 'ctx'), may hold values from -5 to 5
- lengths: int32 [32], P(('dp', 'fsdp')), may hold values from 1 to 1024, as said below
- frozen: bfloat16 [16384, 2048], P(('fsdp', 'ctx')), may hold values from -0.125 to 0.125
- adapter_down: bfloat16 [16, 16384], replicated
- adapter_up: bfloat16 [16, 2048], replicated
Outputs:
- input_grads: bfloat16 [32, 1024, 16384], P(('dp', 'fsdp'), 'ctx')
- grad_down: float32 [16, 16384], replicated
- grad_up: float32 [16, 2048], replicated
Inputs may be any that keep to these rules, and one draw needn't show every extreme that they name: `lengths`: positions below an example's length are real tokens, the rest padding; some example has all 1024 positions live.
All inputs are finite; a program needn't handle non-finite values.
Results may differ from a plain program's by a relative error of at most 0.0033.
Values may be sent and summed in bfloat16 or wider, within the bound.
A program may use at most 128 MiB of HBM per device.

v0:
```python
import math

import jax
import jax.numpy as jnp
from jax import lax
from jax.sharding import PartitionSpec as P

scaling = 2.0


def split_up(value, dim, peers):
    before, after = (value.shape[:dim], value.shape[dim + 1 :])
    return jnp.moveaxis(value.reshape(*before, peers, -1, *after), dim, 0)


def edges_of(length, count):
    unit = 8 if length >= 8 * count else 1
    return [length // unit * k // count * unit for k in range(1, count)]


def joined_along(parts, dim):
    shape = list(parts.shape[1:])
    shape[dim] *= parts.shape[0]
    return jnp.moveaxis(parts, 0, dim).reshape(shape)


def exchange_in_pieces(value, axis, pieces, split_dim, concat_dim):
    parts = split_up(value, split_dim, lax.axis_size(axis))
    cut = max(range(1, max(2, parts.ndim - 1)), key=lambda d: parts.shape[d])
    done = []
    for piece in jnp.split(parts, edges_of(parts.shape[cut], pieces), axis=cut):
        if piece.size:
            done.append(lax.all_to_all(piece, axis, split_axis=0, concat_axis=0, tiled=True))
    return joined_along(jnp.concatenate(done, axis=cut), concat_dim)


def sum_together(arrays, axis, dims):
    peers = lax.axis_size(axis)
    parts = [split_up(a, dim, peers) for a, dim in zip(arrays, dims)]
    lines = jnp.concatenate([b.reshape(peers, -1) for b in parts], axis=1)
    extent = max(16, -(-lines.shape[1] // 1024) * 8)
    lines = jnp.pad(lines, ((0, 0), (0, extent * 128 - lines.shape[1]))).reshape(-1, 128)
    ravelled, at, done = (lax.psum_scatter(lines, axis, tiled=True).reshape(-1), 0, [])
    for b in parts:
        part = b[0]
        done.append(ravelled[at : at + part.size].reshape(part.shape))
        at += part.size
    return tuple(done)


def sent_to_all(value, axis):
    copies = jnp.broadcast_to(value, (lax.axis_size(axis), *value.shape))
    return lax.all_to_all(copies, axis, split_axis=0, concat_axis=0, tiled=True)


def of_everyone(value, axis):
    return sent_to_all(value, axis).sum(axis=0)


def over_pieces(value, axis):
    return lax.all_gather(value, axis).sum(0)


def gather_packed(arrays, axis, dims):
    ravelled = jnp.concatenate([a.reshape(-1) for a in arrays])
    lines, at, done = (lax.all_gather(ravelled, axis), 0, [])
    for a, dim in zip(arrays, dims):
        parts = lines[:, at : at + a.size].reshape(-1, *a.shape)
        done.append(joined_along(parts, dim))
        at += a.size
    return tuple(done)


def contract_last(operand, second):
    return lax.dot_general(
        operand, second, (((1,), (1,)), ((), ())), preferred_element_type=jnp.float32
    )


def contract_first(operand, second):
    return lax.dot_general(
        operand, second, (((0,), (0,)), ((), ())), preferred_element_type=jnp.float32
    )


def adapted_rows(grads_all, lowered_all, down_cols):

    def project(frozen_part, offset):
        return contract_last(grads_all, frozen_part) + scaling * jnp.dot(
            lowered_all, down_cols, preferred_element_type=jnp.float32
        )

    return project


def local(inputs, cotangent, lengths, frozen, adapter_down, adapter_up):
    tok_rows = inputs.shape[1]
    features = inputs.shape[2]
    out_width = cotangent.shape[2]
    rank_count = adapter_down.shape[0]
    block_rows = frozen.shape[0]
    fsdp_count = lax.axis_size("fsdp")
    ctx_count = lax.axis_size("ctx")
    ctx_index = lax.axis_index("ctx")
    position = ctx_index * tok_rows + jnp.arange(tok_rows, dtype=jnp.int32)
    live_mask = position[None, :, None] < lengths[:, None, None]
    masked = jnp.where(live_mask, cotangent, jnp.zeros((), jnp.bfloat16))
    own_rows = inputs.reshape(tok_rows, features)
    own_grads = masked.reshape(tok_rows, out_width)
    projected = contract_last(own_rows, adapter_down).astype(jnp.bfloat16)
    gathered = lax.all_gather(masked, "ctx", axis=1, tiled=True)
    grads_all = gathered.reshape(ctx_count * tok_rows, out_width)
    lowered_all = contract_last(grads_all, adapter_up).astype(jnp.bfloat16)
    lowered = lax.dynamic_slice_in_dim(lowered_all, ctx_index * tok_rows, tok_rows, 0)
    down_cols = adapter_down.reshape(rank_count, fsdp_count, ctx_count, block_rows)
    down_cols = lax.dynamic_index_in_dim(down_cols, ctx_index, 2, keepdims=False)
    down_cols = down_cols.reshape(rank_count, fsdp_count * block_rows)
    project = adapted_rows(grads_all, lowered_all, down_cols)
    local_grads = project(lax.all_gather(frozen, "fsdp", axis=0, tiled=True), jnp.int32(0))
    local_grads = local_grads.astype(jnp.bfloat16).reshape(
        1, ctx_count * tok_rows, fsdp_count, block_rows
    )
    returned = exchange_in_pieces(local_grads, "ctx", 2, 1, 3)
    input_grads = returned.reshape(1, tok_rows, features)
    part_down = scaling * contract_first(lowered, own_rows)
    part_up = scaling * contract_first(projected, own_grads)
    clip_bound = 10.0 * math.sqrt(rank_count * (features + out_width))
    example_count = lax.axis_size("dp") * fsdp_count
    share_down, share_up = sum_together((part_down, part_up), "ctx", (1, 1))
    squared = of_everyone(jnp.sum(share_down * share_down) + jnp.sum(share_up * share_up), "ctx")
    factor = clip_bound / jnp.maximum(jnp.sqrt(squared), clip_bound)
    kept_down, kept_up = (
        over_pieces(factor * share_down, ("dp", "fsdp")),
        over_pieces(factor * share_up, ("dp", "fsdp")),
    )
    sum_down, sum_up = gather_packed((kept_down, kept_up), "ctx", (1, 1))
    return (input_grads, sum_down / example_count, sum_up / example_count)


def solution(mesh):
    placed = (
        P(("dp", "fsdp"), "ctx", None),
        P(("dp", "fsdp"), "ctx", None),
        P(("dp", "fsdp")),
        P(("fsdp", "ctx"), None),
        P(),
        P(),
    )
    return jax.shard_map(
        local,
        mesh=mesh,
        in_specs=placed,
        out_specs=(P(("dp", "fsdp"), "ctx", None), P(), P()),
        check_vma=False,
    )
```

profile of v0, /device:TPU:1, one launch (start us, length us, event | category | flops | bytes accessed | tf_op | source)
XLA Modules:
  0.0 351.4 jit_solution(1828150834598509191)
XLA Ops:
  8.7 1.9 broadcast_select_fusion
  10.7 4.0 %convolution_multiply_fusion.1 = f32[16,2048]{1,0:T(8,128)S(1)} fusion(bf16[16,16384]{1,0:T(8,128)(2,1)} %param.10, bf16[1,128,16384]{2,1,0:T(8,128)(2,1)} %param.6, bf16[1,128,2048]{2,1,0:T(8,128)(2,1)} %broadcast_select_fusion), kind=kOutput, calls=%fused_computation.10 | convolution fusion | flops 75532288 | bytes 5373952 | tf_op jit(solution)/shard_map/dot_general | solution.py:81
  14.8 77.1 %all-gather.6.cloned.1.call-done = bf16[1,1024,2048]{2,1,0:T(8,128)(2,1)} async-done(((bf16[1,128,2048]{2,1,0:T(8,128)(2,1)}), bf16[1,1024,2048]{2,1,0:T(8,128)(2,1)}) %all-gather.6.cloned.1.call-update) | async-done | bytes 4194320 | tf_op jit(solution)/shard_map/all_gather | solution.py:111
  91.8 3.5 %fusion.8 = bf16[1024,16]{0,1:T(8,128)(2,1)S(1)} fusion(bf16[16,2048]{1,0:T(8,128)(2,1)S(1)} %copy-done, bf16[1,1024,2048]{2,1,0:T(8,128)(2,1)} %all-gather.6.cloned.1.call-done), kind=kOutput, calls=%fused_computation.13 | convolution fusion | flops 67125248 | bytes 4292608 | tf_op jit(solution)/shard_map/dot_general | solution.py:75
  95.3 0.7 convolution_multiply_fusion
  96.7 1.2 reshape.108
  98.6 75.5 %reduce-scatter.2.cloned.1.call-done = f32[288,128]{1,0:T(8,128)} async-done(((f32[2304,128]{1,0:T(8,128)}), f32[288,128]{1,0:T(8,128)}) %reduce-scatter.2.cloned.1.call-update) | async-done | bytes 147472 | tf_op jit(solution)/shard_map/reduce_scatter | solution.py:43
  174.0 1.3 multiply_reduce_fusion.1
  175.4 1.5 multiply_reduce_fusion
  178.2 10.7 %all_to_all.16 = f32[8,1,1]{2,1,0:T(1,128)S(1)} all-to-all(f32[8,1,1]{2,1,0:T(1,128)S(1)} %broadcast_in_dim.19), channel_id=1, replica_groups=mesh['dp'=2,'fsdp'=16,'ctx'=8] {'ctx'}, dimensions={0} | all-to-all | bytes 64 | tf_op jit(solution)/shard_map/all_to_all | solution.py:53
  190.3 0.9 slice_multiply_fusion.2
  191.2 0.7 mul.73
  192.5 12.6 %fusion.5 = f32[1024,2048]{1,0:T(8,128)S(1)} fusion(bf16[2048,2048]{1,0:T(8,128)(2,1)} %all-gather.8.cloned.1.call-done, bf16[1,1024,2048]{2,1,0:T(8,128)(2,1)} %all-gather.6.cloned.1.call-done), kind=kOutput, calls=%fused_computation.8 | convolution fusion | flops 8589934592 | bytes 20971520 | tf_op jit(solution)/shard_map/dot_general | solution.py:75
  205.0 1.3 fusion.7
  206.3 1.4 copy.38
  207.8 2.7 fusion.21
  210.5 3.6 %all-to-all-start.1 = ((bf16[8,1,64,16,128]{4,3,2,1,0:T(8,128)(2,1)}), bf16[8,1,64,16,128]{4,3,2,1,0:T(8,128)(2,1)S(1)}, u32[]{:S(2)}, u32[]{:S(2)}) async-start(bf16[8,1,64,16,128]{4,3,2,1,0:T(8,128)(2,1)} %get-tuple-element.13), calls=%async_computation.1 | async-start | bytes 4194304 | tf_op jit(solution)/shard_map/all_to_all | solution.py:33
  214.1 0.7 slice_multiply_fusion.3
  214.9 40.8 %all_gather.23 = f32[32,16,256]{2,1,0:T(8,128)S(1)} all-gather(f32[1,16,256]{2,1,0:T(8,128)S(1)} %mul.76), channel_id=1, replica_groups=mesh['dp'=2,'fsdp'=16,'ctx'=8] {'dp','fsdp'}, dimensions={0}, use_global_device_ids=true | all-gather | bytes 540672 | tf_op jit(solution)/shard_map/all_gather | solution.py:61
  255.8 20.7 %all-gather.10.cloned.1.call-done = f32[32,16,2048]{2,1,0:T(8,128)} async-done(((f32[1,16,2048]{2,1,0:T(8,128)}), f32[32,16,2048]{2,1,0:T(8,128)}) %all-gather.10.cloned.1.call-update) | async-done | bytes 4194320 | tf_op jit(solution)/shard_map/all_gather | solution.py:61
  276.5 2.4 reduce_sum.48
  278.9 0.7 pad_maximum_fusion.2
  279.6 5.8 %all-to-all-start = ((bf16[8,1,64,16,128]{4,3,2,1,0:T(8,128)(2,1)}), bf16[8,1,64,16,128]{4,3,2,1,0:T(8,128)(2,1)}, u32[]{:S(2)}, u32[]{:S(2)}) async-start(bf16[8,1,64,16,128]{4,3,2,1,0:T(8,128)(2,1)} %get-tuple-element.12), calls=%async_computation | async-start | bytes 4194304 | tf_op jit(solution)/shard_map/all_to_all | solution.py:33
  285.4 3.5 %copy.31 = bf16[8,1,64,16,128]{2,4,0,3,1:T(8,128)(2,1)} copy(bf16[8,1,64,16,128]{4,3,2,1,0:T(8,128)(2,1)S(1)} %all-to-all-done.1) | data formatting | bytes 4194304 | tf_op jit(solution)/shard_map/all_to_all | solution.py:33
  289.0 28.8 %all-to-all-done = bf16[8,1,64,16,128]{4,3,2,1,0:T(8,128)(2,1)} async-done(((bf16[8,1,64,16,128]{4,3,2,1,0:T(8,128)(2,1)}), bf16[8,1,64,16,128]{4,3,2,1,0:T(8,128)(2,1)}, u32[]{:S(2)}, u32[]{:S(2)}) %all-to-all-start) | async-done | bytes 2097184 | tf_op jit(solution)/shard_map/all_to_all | solution.py:33
  317.7 4.9 %copy.30 = bf16[8,1,64,16,128]{2,4,0,3,1:T(8,128)(2,1)} copy(bf16[8,1,64,16,128]{4,3,2,1,0:T(8,128)(2,1)} %all-to-all-done) | data formatting | bytes 4194304 | tf_op jit(solution)/shard_map/all_to_all | solution.py:33
  322.7 6.1 %pad_maximum_fusion = bf16[8,1,128,16,128]{2,4,0,3,1:T(8,128)(2,1)} fusion(bf16[8,1,64,16,128]{2,4,0,3,1:T(8,128)(2,1)} %copy.31, bf16[8,1,64,16,128]{2,4,0,3,1:T(8,128)(2,1)} %copy.30), kind=kLoop, calls=%fused_computation.2 | loop fusion | flops 8388608 | bytes 8388608 | tf_op jit(solution)/shard_map/concatenate | solution.py:34
  328.8 6.4 %copy.33 = bf16[1,128,16384]{2,1,0:T(8,128)(2,1)} copy(bf16[1,128,16384]{1,2,0:T(8,128)(2,1)} %bitcast.69) | data formatting | bytes 8388608
  335.2 5.2 %all-gather.12.cloned.1.call-done = f32[294912]{0:T(1024)} async-done(((f32[36864]{0:T(1024)}), f32[294912]{0:T(1024)}) %all-gather.12.cloned.1.call-update) | async-done | bytes 1179664 | tf_op jit(solution)/shard_map/all_gather | solution.py:66
  340.4 1.5 reshape.111
  342.0 1.6 copy.43
  343.6 0.7 copy.44
  (34 shorter events, 2.9 us)
Async XLA Ops:
  8.0 83.8 %copy-start = (bf16[16,2048]{1,0:T(8,128)(2,1)S(1)}, bf16[16,2048]{1,0:T(8,128)(2,1)}, u32[]{:S(2)}) copy-start(bf16[16,2048]{1,0:T(8,128)(2,1)} %param.11) | copy-start | bytes 196612
  8.0 83.8 %all-gather.6.cloned.1.call-start = ((), (), s32[]{:S(2)}) async-start(), calls=%async_computation.4 | async-start | bytes 4718592 | tf_op jit(solution)/shard_map/all_gather | solution.py:111
  10.7 163.3 %reduce-scatter.2.cloned.1.call-start = ((), (), s32[]{:S(2)}) async-start(), calls=%async_computation.6 | async-start | bytes 1327104 | tf_op jit(solution)/shard_map/reduce_scatter | solution.py:43
  91.8 3.5 %copy-start.2 = (bf16[1,128,16384]{2,1,0:T(8,128)(2,1)S(1)}, bf16[1,128,16384]{2,1,0:T(8,128)(2,1)}, u32[]{:S(2)}) copy-start(bf16[1,128,16384]{2,1,0:T(8,128)(2,1)} %param.6) | copy-start | bytes 12582916
  96.0 95.9 %copy-start.3 = (bf16[16,16384]{1,0:T(8,128)(2,1)S(1)}, bf16[16,16384]{1,0:T(8,128)(2,1)}, u32[]{:S(2)}) copy-start(bf16[16,16384]{1,0:T(8,128)(2,1)} %param.10) | copy-start | bytes 1572868
  97.9 94.5 %all-gather.8.cloned.1.call-start = ((), (), s32[]{:S(2)}) async-start(), calls=%async_computation.5 | async-start | bytes 8912896 | tf_op jit(solution)/shard_map/all_gather | solution.py:119
  98.5 177.9 %all-gather.10.cloned.1.call-start = ((), (), s32[]{:S(2)}) async-start(), calls=%async_computation.7 | async-start | bytes 4325376 | tf_op jit(solution)/shard_map/all_gather | solution.py:61
  210.5 69.1 %all-to-all-start.1 = ((bf16[8,1,64,16,128]{4,3,2,1,0:T(8,128)(2,1)}), bf16[8,1,64,16,128]{4,3,2,1,0:T(8,128)(2,1)S(1)}, u32[]{:S(2)}, u32[]{:S(2)}) async-start(bf16[8,1,64,16,128]{4,3,2,1,0:T(8,128)(2,1)} %get-tuple-element.13), calls=%async_computation.1 | async-start | bytes 4194304 | tf_op jit(solution)/shard_map/all_to_all | solution.py:33
  214.1 126.3 %all-gather.12.cloned.1.call-start = ((), (), s32[]{:S(2)}) async-start(), calls=%async_computation.8 | async-start | bytes 1327104 | tf_op jit(solution)/shard_map/all_gather | solution.py:66
  279.6 38.1 %all-to-all-start = ((bf16[8,1,64,16,128]{4,3,2,1,0:T(8,128)(2,1)}), bf16[8,1,64,16,128]{4,3,2,1,0:T(8,128)(2,1)}, u32[]{:S(2)}, u32[]{:S(2)}) async-start(bf16[8,1,64,16,128]{4,3,2,1,0:T(8,128)(2,1)} %get-tuple-element.12), calls=%async_computation | async-start | bytes 4194304 | tf_op jit(solution)/shard_map/all_to_all | solution.py:33
  328.8 15.4 %copy-start.1 = (bf16[16,2048]{1,0:T(8,128)(2,1)S(1)}, bf16[16,2048]{1,0:T(8,128)(2,1)}, u32[]{:S(2)}) copy-start(bf16[16,2048]{1,0:T(8,128)(2,1)} %param.11) | copy-start | bytes 196612
Sparse Core Ops, SparseCore 0:
  12.0 79.7 all-gather.5
  98.1 75.9 reduce-scatter.1
  279.7 60.6 all-gather.11
Sparse Core Ops, SparseCore 1:
  100.3 54.8 all-gather.7
  192.0 84.4 all-gather.9
where the time goes:
time: 353 us; the launch traced here: 351 us
  waiting for transfers between devices  208 us (59%)
  blocking collectives  51.5 us (15%)
  local copies, waits for them, and re-layouts  25.9 us (7%)
  matrix products  22 us (6%)
  between operations  18 us (5%)
  other arithmetic  16.5 us (5%)
  starting transfers between devices  9.63 us (3%)
    all_gather x1, waiting for transfers between devices, local(): gathered = lax.all_gather(masked, 'ctx', axis=1, tiled=True)  77.1 us
    reduce_scatter x1, waiting for transfers between devices, sum_together(): lax.psum_scatter(lines, axis, tiled=True).reshape(-1)  75.5 us
    all_gather x1, blocking collectives, over_pieces(): return lax.all_gather(value, axis).sum(0)  40.8 us
    all_to_all x2, waiting for transfers between devices, exchange_in_pieces(): lax.all_to_all(piece, axis, split_axis=0, concat_axis=0, tiled=True)  28.8 us
    all_gather x1, waiting for transfers between devices, over_pieces(): return lax.all_gather(value, axis).sum(0)  20.7 us
    dot_general x2, matrix products, contract_last(): lax.dot_general(operand, second, (((1,), (1,)), ((), ())), preferred_elem...  16.1 us
    unnamed x17, local copies, waits for them, and re-layouts  10.9 us
    all_to_all x1, blocking collectives, sent_to_all(): return lax.all_to_all(copies, axis, split_axis=0, concat_axis=0, tiled=True)  10.7 us
  transfers between devices with their start and end apart: 7, of which 5 were waited for; matrix products, arithmetic and copies ran while one was open for 15% of the time, Pallas kernels for 0%

commit v1 on v0

v1 whole, which is shorter than its diff:
```python
import functools
import math

import jax
import jax.numpy as jnp
from jax import lax
from jax.experimental import pallas as pl
from jax.experimental.pallas import tpu as pltpu
from jax.sharding import PartitionSpec as P

MESH = pl.DeviceIdType.MESH
BF16, F32 = jnp.bfloat16, jnp.float32
X, Z = 4, 8
OFFSETS = (0, -1, 1, -2, 2, -3, 3, 4)
SEMS = dict(
    local=6, tok=4, tok2=2, mate=7, zp=7, zm=7, cross=8, pair=8, out=64,
    s1=1, s2=3, s3=7, s4=1, s5=7, s6=1, s7=7, s8=3, s9=1, s10=1,
)
BASE, TOTAL = {}, 0
for _name, _count in SEMS.items():
    BASE[_name] = TOTAL
    TOTAL += _count


def last(a, b):
    return lax.dot_general(a, b, (((1,), (1,)), ((), ())), preferred_element_type=F32)


def wrap(value, size):
    return lax.rem(value + size, size)


def body(
    lengths, inp, cot, frz, adn, aup,
    og, gd, gu,
    tok, wts, outs, xin, dn, up, low2,
    part, r1, r2, share, nrm, r4, g8, r5, fin, r6, c7, c8, c9, c10,
    ssem, rsem,
):
    dp, fsdp, ctx = (lax.axis_index(n) for n in ("dp", "fsdp", "ctx"))
    lo, z, c, x, hi = dp, fsdp // 2, lax.rem(fsdp, 2), ctx // 2, lax.rem(ctx, 2)
    rows, width = cot.shape
    half = rows // 2

    def dev(dx=0, dz=0, dc=0, flip_hi=0, flip_lo=0):
        xx, zz = wrap(x + dx, X), wrap(z + dz, Z)
        cc = 1 - c if dc else c
        hh = 1 - hi if flip_hi else hi
        ll = 1 - lo if flip_lo else lo
        return (ll, zz * 2 + cc, xx * 2 + hh)

    peers = [dict(dx=dx, dc=dc) for dx in range(X) for dc in range(2) if dx or dc]
    peers += [dict(dz=dz) for dz in range(1, Z)]
    peers += [dict(dx=dx, flip_hi=1) for dx in range(X)]
    peers += [dict(flip_hi=1, flip_lo=1), dict(flip_lo=1)]

    sent = []

    def send(src, dst, name, i, **to):
        s = BASE[name] + i
        copy = pltpu.make_async_remote_copy(
            src, dst, ssem.at[s], rsem.at[s], device_id=dev(**to), device_id_type=MESH
        )
        copy.start()
        sent.append(copy)

    def got(dst, name, i):
        s = BASE[name] + i
        pltpu.make_async_remote_copy(
            dst, dst, ssem.at[s], rsem.at[s], device_id=dev(dc=1), device_id_type=MESH
        ).wait_recv()

    def local(src, dst, i):
        copy = pltpu.make_async_copy(src, dst, rsem.at[BASE["local"] + i])
        copy.start()
        return copy

    own = x * 2 + c

    def slot(dx, dc=0):
        return wrap(x + dx, X) * 2 + (1 - c if dc else c)

    def wz(d):
        return wrap(z + d, Z)

    cot2, frz2 = cot.reshape(2, half, width), frz.reshape(2, half, width)

    loads = [
        local(aup, up, 0),
        local(cot2, tok.at[own], 1),
        local(adn, dn, 2),
        local(inp, xin, 3),
        local(frz2, wts.at[z, hi], 4),
    ]
    barrier = pltpu.get_barrier_semaphore()
    for p in peers:
        pl.semaphore_signal(barrier, inc=1, device_id=dev(**p), device_id_type=MESH)
    pl.semaphore_wait(barrier, len(peers))

    send(cot2.at[0], tok.at[own, 0], "tok", 0, dx=1)
    send(cot2.at[1], tok.at[own, 1], "tok", 3, dx=-1)
    send(frz2.at[lo], wts.at[z, hi, lo], "zp", 0, dz=1)
    send(frz2.at[lo], wts.at[z, hi, lo], "zm", 0, dz=-1)
    send(frz2.at[lo], wts.at[z, hi, lo], "cross", 0, flip_hi=1, flip_lo=1)
    send(cot2.at[1], tok.at[own, 1], "tok", 1, dx=1)
    send(cot2.at[0], tok.at[own, 0], "tok", 2, dx=-1)
    send(frz2.at[1 - lo], wts.at[z, hi, 1 - lo], "zp", 1, dz=1)
    send(frz2.at[1 - lo], wts.at[z, hi, 1 - lo], "zm", 1, dz=-1)
    send(cot2, tok.at[own], "mate", 0, dc=1)

    def partials():
        for copy in loads[:4]:
            copy.wait()
        position = ctx * rows + lax.broadcasted_iota(jnp.int32, (1, rows), 1)
        live = position < lengths[0]
        mine = tok[own].reshape(rows, width)
        lowered = jnp.where(live, last(up[...], mine), 0.0).astype(BF16)
        proj = jnp.where(live, last(dn[...], xin[...]), 0.0).astype(BF16)
        for j in range(2 * X):
            dcol, ucol = xin.shape[1] // (2 * X), width // (2 * X)
            pd = jnp.dot(lowered, xin[:, j * dcol : (j + 1) * dcol], preferred_element_type=F32)
            part[j % 2, j // 2, :, :dcol] = 2.0 * pd
            pu = jnp.dot(proj, mine[:, j * ucol : (j + 1) * ucol], preferred_element_type=F32)
            part[j % 2, j // 2, :, dcol:] = 2.0 * pu
        send(part.at[1 - hi], r1, "s1", 0, flip_hi=1)

    def stage2():
        got(r1, "s1", 0)
        r1[...] = part[hi] + r1[...]
        for dx in range(1, X):
            send(r1.at[wrap(x + dx, X)], r2.at[dx - 1], "s2", dx - 1, dx=dx)

    def stage3():
        for dx in range(1, X):
            got(r2.at[dx - 1], "s2", dx - 1)
        total = r1[x] + r2[0] + r2[1] + r2[2]
        n = total.shape[1] // 2
        share[0] = total[:, :n]
        share[1] = total[:, n:]
        square = jnp.sum(jnp.sum(total * total, axis=1, keepdims=True), axis=0, keepdims=True)
        nrm[ctx] = jnp.broadcast_to(square, nrm.shape[1:])
        for i in range(1, 2 * X):
            send(nrm.at[ctx], nrm.at[ctx], "s3", i - 1, dx=i // 2, flip_hi=i % 2)

    def stage4():
        for i in range(1, 2 * X):
            src = wrap(x - i // 2, X) * 2 + (1 - hi if i % 2 else hi)
            got(nrm.at[src], "s3", i - 1)
        square = nrm[0]
        for i in range(1, 2 * X):
            square = square + nrm[i]
        bound = 10.0 * math.sqrt(dn.shape[0] * (xin.shape[1] + width))
        factor = (bound / jnp.maximum(jnp.sqrt(square), bound))[:1, :1]
        share[...] = share[...] * factor.reshape(1, 1, 1)
        send(share.at[1 - c], r4, "s4", 0, dc=1)

    def stage5():
        got(r4, "s4", 0)
        both = share[c] + r4[...]
        n = g8.shape[2]
        for o in range(Z):
            if o < 6:
                g8[o] = both[(o % 2) * 8 : (o % 2) * 8 + 8, (o // 2) * n : (o // 2 + 1) * n]
            else:
                g8[o] = jnp.zeros(g8.shape[1:], F32)
        for dz in range(1, Z):
            send(g8.at[wz(dz)], r5.at[dz - 1], "s5", dz - 1, dz=dz)

    def stage6():
        total = g8[z]
        for dz in range(1, Z):
            got(r5.at[dz - 1], "s5", dz - 1)
            total = total + r5[dz - 1]
        fin[...] = total
        send(fin, r6, "s6", 0, flip_lo=1)

    def stage7():
        got(r6, "s6", 0)
        c7[z] = (fin[...] + r6[...]) * (1.0 / 32.0)
        for dz in range(1, Z):
            send(c7.at[z], c7.at[z], "s7", dz - 1, dz=dz)

    def stage8():
        for dz in range(1, Z):
            got(c7.at[wz(-dz)], "s7", dz - 1)
        c8[x] = c7[...]
        for dx in range(1, X):
            send(c7, c8.at[x], "s8", dx - 1, dx=dx)

    def stage9():
        for dx in range(1, X):
            got(c8.at[wrap(x - dx, X)], "s8", dx - 1)
        c9[hi] = c8[...]
        send(c8, c9.at[hi], "s9", 0, flip_hi=1, flip_lo=1)

    def stage10():
        got(c9.at[1 - hi], "s9", 0)
        c10[c] = c9[...]
        send(c9, c10.at[c], "s10", 0, dc=1)

    def finish():
        got(c10.at[1 - c], "s10", 0)
        n = g8.shape[2]
        dcol, ucol = xin.shape[1] // (2 * X), width // (2 * X)
        for j in range(2 * X):
            for cc in range(2):
                for o in range(6):
                    r = slice((o % 2) * 8, (o % 2) * 8 + 8)
                    v = c10[cc, j % 2, j // 2, o]
                    at = cc * 3 * n + (o // 2) * n
                    k = max(0, min(n, dcol - at))
                    if k:
                        gd[r, j * dcol + at : j * dcol + at + k] = v[:, :k]
                    if k < n:
                        u = at + k - dcol
                        gu[r, j * ucol + u : j * ucol + u + n - k] = v[:, k:]

    def weights(k):
        d, which = (k + 1) // 2, (lo if k % 2 else 1 - lo)
        at = wts.at[wz(-d), hi, which]
        got(at, "zp", k - 1)
        if k <= 5:
            send(at, at, "zp", k + 1, dz=1)
        if k % 2:
            send(at, at, "cross", OFFSETS.index(-d if d < 4 else 4), flip_hi=1, flip_lo=1)
        if k == 7:
            which = 1 - lo
        at = wts.at[wz(d), hi, which]
        got(at, "zm", k - 1)
        if k <= 4:
            send(at, at, "zm", k + 1, dz=-1)
        if k == 6:
            send(at, at, "zm", 6, dz=-1)
        if k % 2 and k < 7:
            send(at, at, "cross", OFFSETS.index(d), flip_hi=1, flip_lo=1)

    def across(k):
        at = wts.at[wz(OFFSETS[k - 1]), 1 - hi, 1 - lo]
        got(at, "cross", k - 1)
        send(at, at, "pair", k - 1, flip_lo=1)

    def tokens(k):
        if k == 3:
            moved = ((slot(2), 0, "tok2", 0), (slot(2), 1, "tok2", 1))
        else:
            a, b = (0, 1) if k == 1 else (1, 0)
            moved = ((slot(-1), a, "tok", a), (slot(1), b, "tok", 2 + b))
        for i, (s, part_, name, index) in enumerate(moved):
            at = tok.at[s, part_]
            got(at, name, index)
            if k == 1:
                send(at, at, "tok2", i, dx=1 if i == 0 else -1)
            send(at, at, "mate", 1 + 2 * (k - 1) + i, dc=1)

    def all_tokens():
        got(tok.at[slot(0, 1)], "mate", 0)
        for k in range(1, 4):
            a, b = ((slot(-1, 1), 0), (slot(1, 1), 1)) if k == 1 else ((slot(-1, 1), 1), (slot(1, 1), 0))
            if k == 3:
                a, b = (slot(2, 1), 0), (slot(2, 1), 1)
            got(tok.at[a[0], a[1]], "mate", 1 + 2 * (k - 1))
            got(tok.at[b[0], b[1]], "mate", 2 + 2 * (k - 1))

        @pl.loop(0, 4)
        def _(m):
            t = tok[pl.ds(m * 2, 2)].reshape(2 * rows, width)
            lowered = last(t, up[...]).astype(BF16)
            low2[m] = lowered + lowered

    kept = []

    def product(i):
        if i == 1:
            loads[4].wait()
        got(wts.at[wz(OFFSETS[i - 1]), 1 - hi, lo], "pair", i - 1)
        shard = wz(OFFSETS[i - 1])
        wide = 2 * rows
        at = pl.multiple_of(((shard * 2 + c) * 8 + x * 2) * rows, wide)
        cols = pl.ds(at, wide)
        w = wts.at[shard]

        @pl.loop(0, 4)
        def _(m):
            t = tok[pl.ds(m * 2, 2)].reshape(2 * rows, width)
            value = last(t, w[...].reshape(wide, width))
            value = value + jnp.dot(low2[m], dn[:, cols], preferred_element_type=F32)
            outs[i - 1, pl.ds(m * 2, 2)] = value.astype(BF16).reshape(2, rows, wide)

        for dx in (2, 1, 3, 0):
            for dc in range(2):
                src = outs.at[i - 1, slot(dx, dc)]
                if dx or dc:
                    send(src, og.at[:, cols], "out", (i - 1) * 8 + dx * 2 + dc, dx=dx, dc=dc)
                else:
                    copy = pltpu.make_async_copy(
                        src, og.at[:, cols], rsem.at[BASE["out"] + (i - 1) * 8]
                    )
                    copy.start()
                    kept.append(copy)

    def landed(i):
        shard = wz(OFFSETS[i - 1])
        for dx in range(X):
            for dc in range(2):
                if dx or dc:
                    cc = 1 - c if dc else c
                    at = pl.multiple_of(
                        ((shard * 2 + cc) * 8 + wrap(x - dx, X) * 2) * rows, 2 * rows
                    )
                    got(og.at[:, pl.ds(at, 2 * rows)], "out", (i - 1) * 8 + dx * 2 + dc)

    partials()
    gradients = {2: stage2, 3: stage3, 4: stage4, 5: stage5, 6: stage6, 7: stage7, 8: stage8, 9: stage9}
    for k in range(1, 10):
        if k <= 7:
            weights(k)
        if k <= 8:
            across(k)
        if k <= 3:
            tokens(k)
        if k == 3:
            all_tokens()
            product(1)
        if k >= 3:
            product(k - 1)
        if k in gradients:
            gradients[k]()
    stage10()
    finish()
    for i in range(1, 9):
        landed(i)
    for copy in kept:
        copy.wait()
    for copy in sent:
        copy.wait_send()


def fused(lengths, inp, cot, frz, adn, aup):
    rows, width = cot.shape
    rank, features = adn.shape
    share = (features + width) // (2 * X)
    n = share // 6
    scratch = [
        pltpu.VMEM((2 * X, 2, rows // 2, width), BF16),
        pltpu.VMEM((Z, 2, 2, rows // 2, width), BF16),
        pltpu.VMEM((Z, 2 * X, rows, 2 * rows), BF16),
        pltpu.VMEM((rows, features), BF16),
        pltpu.VMEM((rank, features), BF16),
        pltpu.VMEM((rank, width), BF16),
        pltpu.VMEM((4, 2 * rows, rank), BF16),
        pltpu.VMEM((2, X, rank, share), F32),
        pltpu.VMEM((X, rank, share), F32),
        pltpu.VMEM((X - 1, rank, share), F32),
        pltpu.VMEM((2, rank, share // 2), F32),
        pltpu.VMEM((2 * X, 8, 128), F32),
        pltpu.VMEM((rank, share // 2), F32),
        pltpu.VMEM((Z, 8, n), F32),
        pltpu.VMEM((Z - 1, 8, n), F32),
        pltpu.VMEM((8, n), F32),
        pltpu.VMEM((8, n), F32),
        pltpu.VMEM((Z, 8, n), F32),
        pltpu.VMEM((X, Z, 8, n), F32),
        pltpu.VMEM((2, X, Z, 8, n), F32),
        pltpu.VMEM((2, 2, X, Z, 8, n), F32),
        pltpu.SemaphoreType.DMA((TOTAL,)),
        pltpu.SemaphoreType.DMA((TOTAL,)),
    ]
    anywhere = pl.BlockSpec(memory_space=pl.ANY)
    vmem = pl.BlockSpec(memory_space=pltpu.VMEM)
    return pl.pallas_call(
        body,
        out_shape=(
            jax.ShapeDtypeStruct((rows, features), BF16),
            jax.ShapeDtypeStruct((rank, features), F32),
            jax.ShapeDtypeStruct((rank, width), F32),
        ),
        in_specs=[pl.BlockSpec(memory_space=pltpu.SMEM)] + [anywhere] * 5,
        out_specs=(anywhere, vmem, vmem),
        scratch_shapes=scratch,
        compiler_params=pltpu.CompilerParams(
            collective_id=0, has_side_effects=True, vmem_limit_bytes=56 << 20
        ),
    )(lengths, inp, cot, frz, adn, aup)


def shard(inputs, cotangent, lengths, frozen, adapter_down, adapter_up):
    _, rows, features = inputs.shape
    raw, grad_down, grad_up = fused(
        lengths, inputs[0], cotangent[0], frozen, adapter_down, adapter_up
    )
    position = lax.axis_index("ctx") * rows + jnp.arange(rows, dtype=jnp.int32)
    live = position[:, None] < lengths
    input_grads = jnp.where(live, raw, jnp.zeros((), BF16))
    return input_grads[None], grad_down, grad_up


def solution(mesh):
    rows = P(("dp", "fsdp"), "ctx", None)
    return jax.shard_map(
        shard,
        mesh=mesh,
        in_specs=(rows, rows, P(("dp", "fsdp")), P(("fsdp", "ctx"), None), P(), P()),
        out_specs=(rows, P(), P()),
        check_vma=False,
    )
```

time: 353 us -> 122 us (0.35)
  waiting for transfers between devices: 208 us -> 0 us
  Pallas kernels: 0 us -> 114 us
  blocking collectives: 51.5 us -> 0 us
  local copies, waits for them, and re-layouts: 25.9 us -> 1.63 us
  matrix products: 22 us -> 0 us
  between operations: 18 us -> 1.31 us
  other arithmetic: 16.5 us -> 4.64 us
  starting transfers between devices: 9.63 us -> 0 us
    pallas_call x0 -> x1, Pallas kernels: none -> 114 us  [fused(): pl.pallas_call(body, out_shape=(jax.ShapeDtypeStruct((rows, features), BF...]
    all_gather x4 -> x0, waiting for transfers between devices: 103 us -> none  [the longest x1 77.1 us: local(): gathered = lax.all_gather(masked, 'ctx', axis=1, tiled=True)]
    reduce_scatter x1 -> x0, waiting for transfers between devices: 75.5 us -> none  [sum_together(): lax.psum_scatter(lines, axis, tiled=True).reshape(-1)]
    all_gather x1 -> x0, blocking collectives: 40.8 us -> none  [over_pieces(): return lax.all_gather(value, axis).sum(0)]
    all_to_all x2 -> x0, waiting for transfers between devices: 28.8 us -> none  [exchange_in_pieces(): lax.all_to_all(piece, axis, split_axis=0, concat_axis=0, tiled=True)]
    dot_general x5 -> x0, matrix products: 22 us -> none  [the longest x2 16.1 us: contract_last(): lax.dot_general(operand, second, (((1,), (1,)), ((), ())), preferred_elem...]
    all_to_all x1 -> x0, blocking collectives: 10.7 us -> none  [sent_to_all(): return lax.all_to_all(copies, axis, split_axis=0, concat_axis=0, tiled=True)]
    all_to_all x2 -> x0, starting transfers between devices: 9.42 us -> none  [exchange_in_pieces(): lax.all_to_all(piece, axis, split_axis=0, concat_axis=0, tiled=True)]
  transfers between devices with their start and end apart: 7 -> 0, of which waited for: 5 -> 0; matrix products, arithmetic and copies ran while one was open for 15% -> 0% of each run, Pallas kernels for 0% -> 0%
where the time goes in v1:
time: 122 us
  Pallas kernels  114 us (93%)
  other arithmetic  4.64 us (4%)
  local copies, waits for them, and re-layouts  1.63 us (1%)
  between operations  1.31 us (1%)
    pallas_call x1, Pallas kernels, fused(): pl.pallas_call(body, out_shape=(jax.ShapeDtypeStruct((rows, features), BF...  114 us
    broadcast_in_dim x1, other arithmetic, shard(): return (input_grads[None], grad_down, grad_up)  4.64 us

profile of v1, /device:TPU:1, one launch (start us, length us, event | category | flops | bytes accessed | tf_op | source)
XLA Modules:
  0.0 121.9 jit_solution(3220195737822177119)
XLA Ops:
  1.3 114.4 %shard_map.85 = (bf16[128,16384]{1,0:T(8,128)(2,1)}, f32[16,16384]{1,0:T(8,128)}, f32[16,2048]{1,0:T(8,128)}) custom-call(s32[1]{0:T(128)} %copy.11.lengths, bf16[128,16384]{1,0:T(8,128)(2,1)} %bitcast.6, bf16[128,2048]{1,0:T(8,128)(2,1)} %bitcast.7, bf16[128,2048]{1,0:T(8,128)(2,1)} %frz.1, bf16[16,16384]{1,0:T(8,128)(2,1)} %adn.1, bf16[16,2048]{1,0:T(8,128)(2,1)} %aup.1), custom_call_target="tpu_custom_call" | custom-call | tf_op jit(solution)/shard_map/pallas_call | solution.py:370
  115.7 0.0 copy-start
  115.7 0.0 copy-start.1
  115.7 4.6 %select_bitcast_fusion = bf16[1,128,16384]{2,1,0:T(8,128)(2,1)} fusion(bf16[128,16384]{1,0:T(8,128)(2,1)} %get-tuple-element.6, pred[128]{0:T(512)(128)(4,1)S(1)} %add_compare_fusion), kind=kLoop, calls=%fused_computation | loop fusion | flops 2097152 | bytes 8388736 | tf_op jit(solution)/shard_map/broadcast_in_dim | solution.py:394
  120.3 0.0 copy-done
  120.3 1.0 copy.12
  121.3 0.0 copy-done.1
  121.3 0.7 copy.13
  (1 shorter events, 0.0 us)
Async XLA Ops:
  115.7 4.7 %copy-start = (f32[16,16384]{1,0:T(8,128)S(1)}, f32[16,16384]{1,0:T(8,128)}, u32[]{:S(2)}) copy-start(f32[16,16384]{1,0:T(8,128)} %get-tuple-element.13) | copy-start | bytes 3145732
  115.7 5.6 %copy-start.1 = (f32[16,2048]{1,0:T(8,128)S(1)}, f32[16,2048]{1,0:T(8,128)}, u32[]{:S(2)}) copy-start(f32[16,2048]{1,0:T(8,128)} %get-tuple-element.14) | copy-start | bytes 393220

commit v2 on v1

--- a/solution.py
+++ b/solution.py
@@ -32,9 +32,9 @@
 
 def body(
     lengths, inp, cot, frz, adn, aup,
-    og, gd, gu,
-    tok, wts, outs, xin, dn, up, low2,
-    part, r1, r2, share, nrm, r4, g8, r5, fin, r6, c7, c8, c9, c10,
+    og, gd_out, gu_out,
+    tok, wts, outs, xin, cotv, dn, up, low2,
+    part, part16, q16, r1, r2, share, nrm, r4, g8, r5, fin, r6, c7, c8, c9, c10, gd, gu,
     ssem, rsem,
 ):
     dp, fsdp, ctx = (lax.axis_index(n) for n in ("dp", "fsdp", "ctx"))
@@ -91,6 +91,7 @@
         local(adn, dn, 2),
         local(inp, xin, 3),
         local(frz2, wts.at[z, hi], 4),
+        local(cot, cotv, 5),
     ]
     barrier = pltpu.get_barrier_semaphore()
     for p in peers:
@@ -109,31 +110,39 @@
     send(cot2, tok.at[own], "mate", 0, dc=1)
 
     def partials():
-        for copy in loads[:4]:
-            copy.wait()
+        for i in (0, 5, 2, 3):
+            loads[i].wait()
         position = ctx * rows + lax.broadcasted_iota(jnp.int32, (1, rows), 1)
         live = position < lengths[0]
-        mine = tok[own].reshape(rows, width)
+        mine = cotv[...]
         lowered = jnp.where(live, last(up[...], mine), 0.0).astype(BF16)
         proj = jnp.where(live, last(dn[...], xin[...]), 0.0).astype(BF16)
-        for j in range(2 * X):
-            dcol, ucol = xin.shape[1] // (2 * X), width // (2 * X)
-            pd = jnp.dot(lowered, xin[:, j * dcol : (j + 1) * dcol], preferred_element_type=F32)
-            part[j % 2, j // 2, :, :dcol] = 2.0 * pd
-            pu = jnp.dot(proj, mine[:, j * ucol : (j + 1) * ucol], preferred_element_type=F32)
-            part[j % 2, j // 2, :, dcol:] = 2.0 * pu
-        send(part.at[1 - hi], r1, "s1", 0, flip_hi=1)
+        dcol, ucol = xin.shape[1] // (2 * X), width // (2 * X)
+        for i in range(2 * X):
+            j, keep = (i % X) * 2 + ((1 - hi) if i < X else hi), i >= X
+            a = xin[:, pl.ds(pl.multiple_of(j * dcol, dcol), dcol)]
+            pd = 2.0 * jnp.dot(lowered, a, preferred_element_type=F32)
+            b = cotv[:, pl.ds(pl.multiple_of(j * ucol, ucol), ucol)]
+            pu = 2.0 * jnp.dot(proj, b, preferred_element_type=F32)
+            to = part if keep else part16
+            to[i % X, :, :dcol] = pd.astype(to.dtype)
+            to[i % X, :, dcol:] = pu.astype(to.dtype)
+            if i == X - 1:
+                send(part16, r1, "s1", 0, flip_hi=1)
 
     def stage2():
         got(r1, "s1", 0)
-        r1[...] = part[hi] + r1[...]
+        part[...] = part[...] + r1[...].astype(F32)
+        q16[...] = part[...].astype(BF16)
         for dx in range(1, X):
-            send(r1.at[wrap(x + dx, X)], r2.at[dx - 1], "s2", dx - 1, dx=dx)
+            send(q16.at[wrap(x + dx, X)], r2.at[dx - 1], "s2", dx - 1, dx=dx)
 
     def stage3():
         for dx in range(1, X):
             got(r2.at[dx - 1], "s2", dx - 1)
-        total = r1[x] + r2[0] + r2[1] + r2[2]
+        total = part[x]
+        for i in range(X - 1):
+            total = total + r2[i].astype(F32)
         n = total.shape[1] // 2
         share[0] = total[:, :n]
         share[1] = total[:, n:]
@@ -183,9 +192,9 @@
     def stage8():
         for dz in range(1, Z):
             got(c7.at[wz(-dz)], "s7", dz - 1)
-        c8[x] = c7[...]
+        c8[x] = c7[:6]
         for dx in range(1, X):
-            send(c7, c8.at[x], "s8", dx - 1, dx=dx)
+            send(c7.at[pl.ds(0, 6)], c8.at[x], "s8", dx - 1, dx=dx)
 
     def stage9():
         for dx in range(1, X):
@@ -214,6 +223,11 @@
                     if k < n:
                         u = at + k - dcol
                         gu[r, j * ucol + u : j * ucol + u + n - k] = v[:, k:]
+        step = xin.shape[1] // 4
+        for i in range(4):
+            at = pl.ds(i * step, step)
+            kept.append(local(gd.at[:, at], gd_out.at[:, at], i))
+        kept.append(local(gu, gu_out, 4))
 
     def weights(k):
         d, which = (k + 1) // 2, (lo if k % 2 else 1 - lo)
@@ -252,51 +266,66 @@
                 send(at, at, "tok2", i, dx=1 if i == 0 else -1)
             send(at, at, "mate", 1 + 2 * (k - 1) + i, dc=1)
 
-    def all_tokens():
-        got(tok.at[slot(0, 1)], "mate", 0)
-        for k in range(1, 4):
-            a, b = ((slot(-1, 1), 0), (slot(1, 1), 1)) if k == 1 else ((slot(-1, 1), 1), (slot(1, 1), 0))
-            if k == 3:
-                a, b = (slot(2, 1), 0), (slot(2, 1), 1)
-            got(tok.at[a[0], a[1]], "mate", 1 + 2 * (k - 1))
-            got(tok.at[b[0], b[1]], "mate", 2 + 2 * (k - 1))
-
-        @pl.loop(0, 4)
-        def _(m):
-            t = tok[pl.ds(m * 2, 2)].reshape(2 * rows, width)
+    kept = []
+
+    def chunk(i, dx, cols):
+        shard, xx = wz(OFFSETS[i - 1]), wrap(x + dx, X)
+        t = tok[pl.ds(xx * 2, 2)].reshape(2 * rows, width)
+        if i == 1:
             lowered = last(t, up[...]).astype(BF16)
-            low2[m] = lowered + lowered
-
-    kept = []
+            low2[xx] = lowered + lowered
+        value = last(t, wts[shard].reshape(2 * rows, width))
+        value = value + jnp.dot(low2[xx], dn[:, cols], preferred_element_type=F32)
+        outs[i - 1, pl.ds(xx * 2, 2)] = value.astype(BF16).reshape(2, rows, 2 * rows)
+
+    def deliver(i, dx, dc, cols):
+        s = BASE["out"] + (i - 1) * 8 + dx * 2 + dc
+        return pltpu.make_async_remote_copy(
+            outs.at[i - 1, slot(dx, dc)], og.at[:, cols], ssem.at[s], rsem.at[s],
+            device_id=dev(dx=dx, dc=dc), device_id_type=MESH,
+        )
 
     def product(i):
         if i == 1:
+            loads[1].wait()
             loads[4].wait()
-        got(wts.at[wz(OFFSETS[i - 1]), 1 - hi, lo], "pair", i - 1)
         shard = wz(OFFSETS[i - 1])
-        wide = 2 * rows
-        at = pl.multiple_of(((shard * 2 + c) * 8 + x * 2) * rows, wide)
-        cols = pl.ds(at, wide)
-        w = wts.at[shard]
-
-        @pl.loop(0, 4)
-        def _(m):
-            t = tok[pl.ds(m * 2, 2)].reshape(2 * rows, width)
-            value = last(t, w[...].reshape(wide, width))
-            value = value + jnp.dot(low2[m], dn[:, cols], preferred_element_type=F32)
-            outs[i - 1, pl.ds(m * 2, 2)] = value.astype(BF16).reshape(2, rows, wide)
-
-        for dx in (2, 1, 3, 0):
+        got(wts.at[shard, 1 - hi, lo], "pair", i - 1)
+        at = pl.multiple_of(((shard * 2 + c) * 8 + x * 2) * rows, 2 * rows)
+        cols = pl.ds(at, 2 * rows)
+        if i == 1:
+            for k, (d, halves) in enumerate(((-1, (0, 1)), (1, (1, 0)))):
+                got(tok.at[slot(d, 1), halves[0]], "mate", 1 + k)
+                got(tok.at[slot(d, 1), halves[1]], "mate", 3 + k)
+            for dx in (1, 3, 2, 0):
+                if dx == 2:
+                    got(tok.at[slot(2, 1), 0], "mate", 5)
+                    got(tok.at[slot(2, 1), 1], "mate", 6)
+                if dx == 0:
+                    got(tok.at[slot(0, 1)], "mate", 0)
+                chunk(i, dx, cols)
+                if dx:
+                    for dc in range(2):
+                        deliver(i, dx, dc, cols).start()
+        else:
+
+            @pl.loop(0, 3)
+            def _(t):
+                dx = 2 - t + 3 * (t // 2)
+                chunk(i, dx, cols)
+                for dc in range(2):
+                    deliver(i, dx, dc, cols).start()
+
+            chunk(i, 0, cols)
+        for dx in range(1, X):
             for dc in range(2):
-                src = outs.at[i - 1, slot(dx, dc)]
-                if dx or dc:
-                    send(src, og.at[:, cols], "out", (i - 1) * 8 + dx * 2 + dc, dx=dx, dc=dc)
-                else:
-                    copy = pltpu.make_async_copy(
-                        src, og.at[:, cols], rsem.at[BASE["out"] + (i - 1) * 8]
-                    )
-                    copy.start()
-                    kept.append(copy)
+                sent.append(deliver(i, dx, dc, cols))
+        send(outs.at[i - 1, slot(0, 1)], og.at[:, cols], "out", (i - 1) * 8 + 1, dc=1)
+        copy = pltpu.make_async_copy(
+            outs.at[i - 1, own], og.at[:, cols], rsem.at[BASE["out"] + (i - 1) * 8]
+        )
+        copy.start()
+        kept.append(copy)
 
     def landed(i):
         shard = wz(OFFSETS[i - 1])
@@ -310,22 +339,24 @@
                     got(og.at[:, pl.ds(at, 2 * rows)], "out", (i - 1) * 8 + dx * 2 + dc)
 
     partials()
-    gradients = {2: stage2, 3: stage3, 4: stage4, 5: stage5, 6: stage6, 7: stage7, 8: stage8, 9: stage9}
-    for k in range(1, 10):
-        if k <= 7:
-            weights(k)
+    tokens(1)
+    weights(1)
+    stage2()
+    tokens(2)
+    across(1)
+    weights(2)
+    after = {1: stage4, 2: stage5, 3: stage6, 4: stage7, 5: stage8, 7: stage9, 8: stage10}
+    for k in range(2, 10):
         if k <= 8:
             across(k)
-        if k <= 3:
-            tokens(k)
-        if k == 3:
-            all_tokens()
-            product(1)
-        if k >= 3:
-            product(k - 1)
-        if k in gradients:
-            gradients[k]()
-    stage10()
+        if k <= 6:
+            weights(k + 1)
+        if k == 2:
+            tokens(3)
+            stage3()
+        product(k - 1)
+        if k - 1 in after:
+            after[k - 1]()
     finish()
     for i in range(1, 9):
         landed(i)
@@ -345,12 +376,15 @@
         pltpu.VMEM((Z, 2, 2, rows // 2, width), BF16),
         pltpu.VMEM((Z, 2 * X, rows, 2 * rows), BF16),
         pltpu.VMEM((rows, features), BF16),
+        pltpu.VMEM((rows, width), BF16),
         pltpu.VMEM((rank, features), BF16),
         pltpu.VMEM((rank, width), BF16),
         pltpu.VMEM((4, 2 * rows, rank), BF16),
-        pltpu.VMEM((2, X, rank, share), F32),
         pltpu.VMEM((X, rank, share), F32),
-        pltpu.VMEM((X - 1, rank, share), F32),
+        pltpu.VMEM((X, rank, share), BF16),
+        pltpu.VMEM((X, rank, share), BF16),
+        pltpu.VMEM((X, rank, share), BF16),
+        pltpu.VMEM((X - 1, rank, share), BF16),
         pltpu.VMEM((2, rank, share // 2), F32),
         pltpu.VMEM((2 * X, 8, 128), F32),
         pltpu.VMEM((rank, share // 2), F32),
@@ -359,14 +393,16 @@
         pltpu.VMEM((8, n), F32),
         pltpu.VMEM((8, n), F32),
         pltpu.VMEM((Z, 8, n), F32),
-        pltpu.VMEM((X, Z, 8, n), F32),
-        pltpu.VMEM((2, X, Z, 8, n), F32),
-        pltpu.VMEM((2, 2, X, Z, 8, n), F32),
+        pltpu.VMEM((X, 6, 8, n), F32),
+        pltpu.VMEM((2, X, 6, 8, n), F32),
+        pltpu.VMEM((2, 2, X, 6, 8, n), F32),
+        pltpu.VMEM((rank, features), F32),
+        pltpu.VMEM((rank, width), F32),
         pltpu.SemaphoreType.DMA((TOTAL,)),
         pltpu.SemaphoreType.DMA((TOTAL,)),
     ]
     anywhere = pl.BlockSpec(memory_space=pl.ANY)
-    vmem = pl.BlockSpec(memory_space=pltpu.VMEM)
+    hbm = pl.BlockSpec(memory_space=pltpu.HBM)
     return pl.pallas_call(
         body,
         out_shape=(
@@ -374,13 +410,13 @@
             jax.ShapeDtypeStruct((rank, features), F32),
             jax.ShapeDtypeStruct((rank, width), F32),
         ),
-        in_specs=[pl.BlockSpec(memory_space=pltpu.SMEM)] + [anywhere] * 5,
-        out_specs=(anywhere, vmem, vmem),
+        in_specs=[pl.BlockSpec(memory_space=pltpu.SMEM)] + [hbm] * 5,
+        out_specs=(anywhere, anywhere, anywhere),
         scratch_shapes=scratch,
         compiler_params=pltpu.CompilerParams(
-            collective_id=0, has_side_effects=True, vmem_limit_bytes=56 << 20
+            collective_id=0, has_side_effects=True, vmem_limit_bytes=44 << 20
         ),
-    )(lengths, inp, cot, frz, adn, aup)
+    )(lengths, *(pltpu.with_memory_space_constraint(a, pltpu.HBM) for a in (inp, cot, frz, adn, aup)))
 
 
 def shard(inputs, cotangent, lengths, frozen, adapter_down, adapter_up):

time: 122 us -> 91.7 us (0.75)
  Pallas kernels: 114 us -> 86.3 us
  other arithmetic: 4.64 us -> 2.36 us
    pallas_call x1, Pallas kernels: 114 us -> 86.3 us  [fused(): pl.pallas_call(body, out_shape=(jax.ShapeDtypeStruct((rows, features), BF...]
    broadcast_in_dim x1, other arithmetic: 4.64 us -> 2.36 us  [shard(): return (input_grads[None], grad_down, grad_up)]
where the time goes in v2:
time: 91.7 us; the launch traced here: 91.6 us
  Pallas kernels  86.3 us (94%)
  other arithmetic  2.36 us (3%)
  local copies, waits for them, and re-layouts  1.62 us (2%)
  between operations  1.29 us (1%)
    pallas_call x1, Pallas kernels, fused(): pl.pallas_call(body, out_shape=(jax.ShapeDtypeStruct((rows, features), BF...  86.3 us
    broadcast_in_dim x1, other arithmetic, shard(): return (input_grads[None], grad_down, grad_up)  2.36 us

profile of v2, /device:TPU:1, one launch (start us, length us, event | category | flops | bytes accessed | tf_op | source)
XLA Modules:
  0.0 91.6 jit_solution(16643569875111491682)
XLA Ops:
  1.3 86.3 %shard_map.85 = (bf16[128,16384]{1,0:T(8,128)(2,1)S(1)}, f32[16,16384]{1,0:T(8,128)S(1)}, f32[16,2048]{1,0:T(8,128)S(1)}) custom-call(s32[1]{0:T(128)} %copy.11.lengths, bf16[128,16384]{1,0:T(8,128)(2,1)} %bitcast.6, bf16[128,2048]{1,0:T(8,128)(2,1)} %bitcast.7, bf16[128,2048]{1,0:T(8,128)(2,1)} %frz.1, bf16[16,16384]{1,0:T(8,128)(2,1)} %adn.1, ...), custom_call_target="tpu_custom_call" | custom-call | tf_op jit(solution)/shard_map/pallas_call | solution.py:406
  87.6 2.4 %select_bitcast_fusion = bf16[1,128,16384]{2,1,0:T(8,128)(2,1)} fusion(bf16[128,16384]{1,0:T(8,128)(2,1)S(1)} %get-tuple-element.6, pred[128]{0:T(512)(128)(4,1)S(1)} %add_compare_fusion), kind=kLoop, calls=%fused_computation | loop fusion | flops 2097152 | bytes 8388736 | tf_op jit(solution)/shard_map/broadcast_in_dim | solution.py:430
  90.0 1.0 %copy.12 = f32[16,16384]{1,0:T(8,128)} copy(f32[16,16384]{1,0:T(8,128)S(1)} %get-tuple-element.13) | data formatting | bytes 2097152
  90.9 0.7 copy.13
  (1 shorter events, 0.0 us)

commit v3 on v2

--- a/solution.py
+++ b/solution.py
@@ -13,7 +13,7 @@
 X, Z = 4, 8
 OFFSETS = (0, -1, 1, -2, 2, -3, 3, 4)
 SEMS = dict(
-    local=6, tok=4, tok2=2, mate=7, zp=7, zm=7, cross=8, pair=8, out=64,
+    local=6, tok=4, tok2=2, mate=7, zp=7, zm=7, cross=8, pair=8, out=8, outs=1,
     s1=1, s2=3, s3=7, s4=1, s5=7, s6=1, s7=7, s8=3, s9=1, s10=1,
 )
 BASE, TOTAL = {}, 0
@@ -34,7 +34,7 @@
     lengths, inp, cot, frz, adn, aup,
     og, gd_out, gu_out,
     tok, wts, outs, xin, cotv, dn, up, low2,
-    part, part16, q16, r1, r2, share, nrm, r4, g8, r5, fin, r6, c7, c8, c9, c10, gd, gu,
+    part, part16, q16, r1, r2, share, nrm, r4, r6, g8, r5, c7, c8, c9, c10, gd, gu,
     ssem, rsem,
 ):
     dp, fsdp, ctx = (lax.axis_index(n) for n in ("dp", "fsdp", "ctx"))
@@ -165,7 +165,12 @@
 
     def stage5():
         got(r4, "s4", 0)
-        both = share[c] + r4[...]
+        share[c] = share[c] + r4[...]
+        send(share.at[c], r6, "s6", 0, flip_lo=1)
+
+    def stage6():
+        got(r6, "s6", 0)
+        both = share[c] + r6[...]
         n = g8.shape[2]
         for o in range(Z):
             if o < 6:
@@ -175,17 +180,12 @@
         for dz in range(1, Z):
             send(g8.at[wz(dz)], r5.at[dz - 1], "s5", dz - 1, dz=dz)
 
-    def stage6():
+    def stage7():
         total = g8[z]
         for dz in range(1, Z):
             got(r5.at[dz - 1], "s5", dz - 1)
             total = total + r5[dz - 1]
-        fin[...] = total
-        send(fin, r6, "s6", 0, flip_lo=1)
-
-    def stage7():
-        got(r6, "s6", 0)
-        c7[z] = (fin[...] + r6[...]) * (1.0 / 32.0)
+        c7[z] = total * (1.0 / 32.0)
         for dz in range(1, Z):
             send(c7.at[z], c7.at[z], "s7", dz - 1, dz=dz)
 
@@ -262,24 +262,37 @@
         for i, (s, part_, name, index) in enumerate(moved):
             at = tok.at[s, part_]
             got(at, name, index)
+            send(at, at, "mate", 1 + 2 * (k - 1) + i, dc=1)
             if k == 1:
                 send(at, at, "tok2", i, dx=1 if i == 0 else -1)
-            send(at, at, "mate", 1 + 2 * (k - 1) + i, dc=1)
 
     kept = []
+
+    def lower(dx):
+        if dx == 0:
+            loads[1].wait()
+            got(tok.at[slot(0, 1)], "mate", 0)
+        elif dx == 2:
+            got(tok.at[slot(2, 1), 0], "mate", 5)
+            got(tok.at[slot(2, 1), 1], "mate", 6)
+        else:
+            k = 0 if dx == 3 else 1
+            got(tok.at[slot(dx, 1), k], "mate", 1 + k)
+            got(tok.at[slot(dx, 1), 1 - k], "mate", 3 + k)
+        xx = wrap(x + dx, X)
+        t = tok[pl.ds(xx * 2, 2)].reshape(2 * rows, width)
+        lowered = last(t, up[...]).astype(BF16)
+        low2[xx] = lowered + lowered
 
     def chunk(i, dx, cols):
         shard, xx = wz(OFFSETS[i - 1]), wrap(x + dx, X)
         t = tok[pl.ds(xx * 2, 2)].reshape(2 * rows, width)
-        if i == 1:
-            lowered = last(t, up[...]).astype(BF16)
-            low2[xx] = lowered + lowered
         value = last(t, wts[shard].reshape(2 * rows, width))
         value = value + jnp.dot(low2[xx], dn[:, cols], preferred_element_type=F32)
         outs[i - 1, pl.ds(xx * 2, 2)] = value.astype(BF16).reshape(2, rows, 2 * rows)
 
     def deliver(i, dx, dc, cols):
-        s = BASE["out"] + (i - 1) * 8 + dx * 2 + dc
+        s = BASE["outs"]
         return pltpu.make_async_remote_copy(
             outs.at[i - 1, slot(dx, dc)], og.at[:, cols], ssem.at[s], rsem.at[s],
             device_id=dev(dx=dx, dc=dc), device_id_type=MESH,
@@ -287,22 +300,15 @@
 
     def product(i):
         if i == 1:
-            loads[1].wait()
             loads[4].wait()
         shard = wz(OFFSETS[i - 1])
         got(wts.at[shard, 1 - hi, lo], "pair", i - 1)
         at = pl.multiple_of(((shard * 2 + c) * 8 + x * 2) * rows, 2 * rows)
         cols = pl.ds(at, 2 * rows)
         if i == 1:
-            for k, (d, halves) in enumerate(((-1, (0, 1)), (1, (1, 0)))):
-                got(tok.at[slot(d, 1), halves[0]], "mate", 1 + k)
-                got(tok.at[slot(d, 1), halves[1]], "mate", 3 + k)
             for dx in (1, 3, 2, 0):
                 if dx == 2:
-                    got(tok.at[slot(2, 1), 0], "mate", 5)
-                    got(tok.at[slot(2, 1), 1], "mate", 6)
-                if dx == 0:
-                    got(tok.at[slot(0, 1)], "mate", 0)
+                    lower(2)
                 chunk(i, dx, cols)
                 if dx:
                     for dc in range(2):
@@ -317,26 +323,12 @@
                     deliver(i, dx, dc, cols).start()
 
             chunk(i, 0, cols)
-        for dx in range(1, X):
-            for dc in range(2):
-                sent.append(deliver(i, dx, dc, cols))
-        send(outs.at[i - 1, slot(0, 1)], og.at[:, cols], "out", (i - 1) * 8 + 1, dc=1)
+        deliver(i, 0, 1, cols).start()
         copy = pltpu.make_async_copy(
-            outs.at[i - 1, own], og.at[:, cols], rsem.at[BASE["out"] + (i - 1) * 8]
+            outs.at[i - 1, own], og.at[:, cols], rsem.at[BASE["out"] + i - 1]
         )
         copy.start()
         kept.append(copy)
-
-    def landed(i):
-        shard = wz(OFFSETS[i - 1])
-        for dx in range(X):
-            for dc in range(2):
-                if dx or dc:
-                    cc = 1 - c if dc else c
-                    at = pl.multiple_of(
-                        ((shard * 2 + cc) * 8 + wrap(x - dx, X) * 2) * rows, 2 * rows
-                    )
-                    got(og.at[:, pl.ds(at, 2 * rows)], "out", (i - 1) * 8 + dx * 2 + dc)
 
     partials()
     tokens(1)
@@ -345,23 +337,47 @@
     tokens(2)
     across(1)
     weights(2)
-    after = {1: stage4, 2: stage5, 3: stage6, 4: stage7, 5: stage8, 7: stage9, 8: stage10}
-    for k in range(2, 10):
-        if k <= 8:
-            across(k)
-        if k <= 6:
-            weights(k + 1)
-        if k == 2:
-            tokens(3)
-            stage3()
-        product(k - 1)
-        if k - 1 in after:
-            after[k - 1]()
+    lower(0)
+    lower(1)
+    lower(3)
+    across(2)
+    weights(3)
+    tokens(3)
+    stage3()
+    product(1)
+    across(3)
+    weights(4)
+    stage4()
+    product(2)
+    stage5()
+    weights(5)
+    across(4)
+    product(3)
+    stage6()
+    weights(6)
+    across(5)
+    product(4)
+    stage7()
+    weights(7)
+    across(6)
+    product(5)
+    stage8()
+    across(7)
+    product(6)
+    across(8)
+    product(7)
+    stage9()
+    product(8)
+    stage10()
     finish()
-    for i in range(1, 9):
-        landed(i)
     for copy in kept:
         copy.wait()
+    s = BASE["outs"]
+    moved = outs.at[pl.ds(0, 7)]
+    every = pltpu.make_async_remote_copy(
+        moved, moved, ssem.at[s], rsem.at[s], device_id=dev(dc=1), device_id_type=MESH
+    )
+    every.wait()
     for copy in sent:
         copy.wait_send()
 
@@ -388,10 +404,9 @@
         pltpu.VMEM((2, rank, share // 2), F32),
         pltpu.VMEM((2 * X, 8, 128), F32),
         pltpu.VMEM((rank, share // 2), F32),
+        pltpu.VMEM((rank, share // 2), F32),
         pltpu.VMEM((Z, 8, n), F32),
         pltpu.VMEM((Z - 1, 8, n), F32),
-        pltpu.VMEM((8, n), F32),
-        pltpu.VMEM((8, n), F32),
         pltpu.VMEM((Z, 8, n), F32),
         pltpu.VMEM((X, 6, 8, n), F32),
         pltpu.VMEM((2, X, 6, 8, n), F32),

time: 91.7 us -> 90.2 us (0.984)
  Pallas kernels: 86.3 us -> 84.9 us
    pallas_call x1, Pallas kernels: 86.3 us -> 84.9 us  [fused(): pl.pallas_call(body, out_shape=(jax.ShapeDtypeStruct((rows, features), BF...]
where the time goes in v3:
time: 90.2 us
  Pallas kernels  84.9 us (94%)
  other arithmetic  2.36 us (3%)
  local copies, waits for them, and re-layouts  1.62 us (2%)
  between operations  1.29 us (1%)
    pallas_call x1, Pallas kernels, fused(): pl.pallas_call(body, out_shape=(jax.ShapeDtypeStruct((rows, features), BF...  84.9 us
    broadcast_in_dim x1, other arithmetic, shard(): return (input_grads[None], grad_down, grad_up)  2.36 us

profile of v3, /device:TPU:1, one launch (start us, length us, event | category | flops | bytes accessed | tf_op | source)
XLA Modules:
  0.0 90.2 jit_solution(6486587355669321238)
XLA Ops:
  1.3 84.9 %shard_map.85 = (bf16[128,16384]{1,0:T(8,128)(2,1)S(1)}, f32[16,16384]{1,0:T(8,128)S(1)}, f32[16,2048]{1,0:T(8,128)S(1)}) custom-call(s32[1]{0:T(128)} %copy.11.lengths, bf16[128,16384]{1,0:T(8,128)(2,1)} %bitcast.6, bf16[128,2048]{1,0:T(8,128)(2,1)} %bitcast.7, bf16[128,2048]{1,0:T(8,128)(2,1)} %frz.1, bf16[16,16384]{1,0:T(8,128)(2,1)} %adn.1, ...), custom_call_target="tpu_custom_call" | custom-call | tf_op jit(solution)/shard_map/pallas_call | solution.py:421
  86.2 2.4 %select_bitcast_fusion = bf16[1,128,16384]{2,1,0:T(8,128)(2,1)} fusion(bf16[128,16384]{1,0:T(8,128)(2,1)S(1)} %get-tuple-element.6, pred[128]{0:T(512)(128)(4,1)S(1)} %add_compare_fusion), kind=kLoop, calls=%fused_computation | loop fusion | flops 2097152 | bytes 8388736 | tf_op jit(solution)/shard_map/broadcast_in_dim | solution.py:445
  88.5 1.0 %copy.12 = f32[16,16384]{1,0:T(8,128)} copy(f32[16,16384]{1,0:T(8,128)S(1)} %get-tuple-element.13) | data formatting | bytes 2097152
  89.5 0.7 copy.13
  (1 shorter events, 0.0 us)

commit v4 on v3

--- a/solution.py
+++ b/solution.py
@@ -13,13 +13,15 @@
 X, Z = 4, 8
 OFFSETS = (0, -1, 1, -2, 2, -3, 3, 4)
 SEMS = dict(
-    local=6, tok=4, tok2=2, mate=7, zp=7, zm=7, cross=8, pair=8, out=8, outs=1,
-    s1=1, s2=3, s3=7, s4=1, s5=7, s6=1, s7=7, s8=3, s9=1, s10=1,
+    local=6, tok=4, tok2=2, mate=7, zp=7, zm=7, cross=8, pair=8, out=1, outs=1,
+    s1=1, s2=1, s3=1, s4=1, s5=1, s6=1, s7=1, s8=1, s9=1, s10=1,
 )
 BASE, TOTAL = {}, 0
 for _name, _count in SEMS.items():
     BASE[_name] = TOTAL
     TOTAL += _count
+GROUP = dict(tok=0, tok2=0, mate=0, zp=1, zm=1, cross=1, pair=1, outs=2)
+GROUP.update({f"s{i}": i + 2 for i in range(1, 11)})
 
 
 def last(a, b):
@@ -54,21 +56,23 @@
     peers += [dict(dx=dx, flip_hi=1) for dx in range(X)]
     peers += [dict(flip_hi=1, flip_lo=1), dict(flip_lo=1)]
 
-    sent = []
-
     def send(src, dst, name, i, **to):
-        s = BASE[name] + i
-        copy = pltpu.make_async_remote_copy(
-            src, dst, ssem.at[s], rsem.at[s], device_id=dev(**to), device_id_type=MESH
-        )
-        copy.start()
-        sent.append(copy)
-
-    def got(dst, name, i):
-        s = BASE[name] + i
+        r = BASE[name] + min(i, SEMS[name] - 1)
         pltpu.make_async_remote_copy(
-            dst, dst, ssem.at[s], rsem.at[s], device_id=dev(dc=1), device_id_type=MESH
+            src, dst, ssem.at[GROUP[name]], rsem.at[r], device_id=dev(**to), device_id_type=MESH
+        ).start()
+
+    def got(dst, name, i=0):
+        pltpu.make_async_remote_copy(
+            dst, dst, ssem.at[GROUP[name]], rsem.at[BASE[name] + i],
+            device_id=dev(dc=1), device_id_type=MESH,
         ).wait_recv()
+
+    def left(src, name):
+        pltpu.make_async_remote_copy(
+            src, src, ssem.at[GROUP[name]], rsem.at[BASE[name]],
+            device_id=dev(dc=1), device_id_type=MESH,
+        ).wait_send()
 
     def local(src, dst, i):
         copy = pltpu.make_async_copy(src, dst, rsem.at[BASE["local"] + i])
@@ -138,8 +142,7 @@
             send(q16.at[wrap(x + dx, X)], r2.at[dx - 1], "s2", dx - 1, dx=dx)
 
     def stage3():
-        for dx in range(1, X):
-            got(r2.at[dx - 1], "s2", dx - 1)
+        got(r2, "s2")
         total = part[x]
         for i in range(X - 1):
             total = total + r2[i].astype(F32)
@@ -152,9 +155,7 @@
             send(nrm.at[ctx], nrm.at[ctx], "s3", i - 1, dx=i // 2, flip_hi=i % 2)
 
     def stage4():
-        for i in range(1, 2 * X):
-            src = wrap(x - i // 2, X) * 2 + (1 - hi if i % 2 else hi)
-            got(nrm.at[src], "s3", i - 1)
+        got(nrm.at[pl.ds(0, 7)], "s3")
         square = nrm[0]
         for i in range(1, 2 * X):
             square = square + nrm[i]
@@ -181,24 +182,22 @@
             send(g8.at[wz(dz)], r5.at[dz - 1], "s5", dz - 1, dz=dz)
 
     def stage7():
+        got(r5, "s5")
         total = g8[z]
         for dz in range(1, Z):
-            got(r5.at[dz - 1], "s5", dz - 1)
             total = total + r5[dz - 1]
         c7[z] = total * (1.0 / 32.0)
         for dz in range(1, Z):
             send(c7.at[z], c7.at[z], "s7", dz - 1, dz=dz)
 
     def stage8():
-        for dz in range(1, Z):
-            got(c7.at[wz(-dz)], "s7", dz - 1)
+        got(c7.at[pl.ds(0, 7)], "s7")
         c8[x] = c7[:6]
         for dx in range(1, X):
             send(c7.at[pl.ds(0, 6)], c8.at[x], "s8", dx - 1, dx=dx)
 
     def stage9():
-        for dx in range(1, X):
-            got(c8.at[wrap(x - dx, X)], "s8", dx - 1)
+        got(c8.at[pl.ds(0, 3)], "s8")
         c9[hi] = c8[...]
         send(c8, c9.at[hi], "s9", 0, flip_hi=1, flip_lo=1)
 
@@ -292,9 +291,9 @@
         outs[i - 1, pl.ds(xx * 2, 2)] = value.astype(BF16).reshape(2, rows, 2 * rows)
 
     def deliver(i, dx, dc, cols):
-        s = BASE["outs"]
         return pltpu.make_async_remote_copy(
-            outs.at[i - 1, slot(dx, dc)], og.at[:, cols], ssem.at[s], rsem.at[s],
+            outs.at[i - 1, slot(dx, dc)], og.at[:, cols],
+            ssem.at[GROUP["outs"]], rsem.at[BASE["outs"]],
             device_id=dev(dx=dx, dc=dc), device_id_type=MESH,
         )
 
@@ -324,11 +323,7 @@
 
             chunk(i, 0, cols)
         deliver(i, 0, 1, cols).start()
-        copy = pltpu.make_async_copy(
-            outs.at[i - 1, own], og.at[:, cols], rsem.at[BASE["out"] + i - 1]
-        )
-        copy.start()
-        kept.append(copy)
+        pltpu.make_async_copy(outs.at[i - 1, own], og.at[:, cols], rsem.at[BASE["out"]]).start()
 
     partials()
     tokens(1)
@@ -372,14 +367,22 @@
     finish()
     for copy in kept:
         copy.wait()
-    s = BASE["outs"]
+    pltpu.make_async_copy(outs.at[0], outs.at[0], rsem.at[BASE["out"]]).wait()
     moved = outs.at[pl.ds(0, 7)]
-    every = pltpu.make_async_remote_copy(
-        moved, moved, ssem.at[s], rsem.at[s], device_id=dev(dc=1), device_id_type=MESH
-    )
-    every.wait()
-    for copy in sent:
-        copy.wait_send()
+    got(moved, "outs")
+    left(moved, "outs")
+    left(tok.at[pl.ds(0, 7)], "tok")
+    left(wts.reshape(4 * Z, half, width).at[pl.ds(0, 30)], "zp")
+    left(part16, "s1")
+    left(r2, "s2")
+    left(nrm.at[pl.ds(0, 7)], "s3")
+    left(r4, "s4")
+    left(r5, "s5")
+    left(r6, "s6")
+    left(c7.at[pl.ds(0, 7)], "s7")
+    left(c8.at[pl.ds(0, 3)], "s8")
+    left(c8, "s9")
+    left(c9, "s10")
 
 
 def fused(lengths, inp, cot, frz, adn, aup):
@@ -413,7 +416,7 @@
         pltpu.VMEM((2, 2, X, 6, 8, n), F32),
         pltpu.VMEM((rank, features), F32),
         pltpu.VMEM((rank, width), F32),
-        pltpu.SemaphoreType.DMA((TOTAL,)),
+        pltpu.SemaphoreType.DMA((13,)),
         pltpu.SemaphoreType.DMA((TOTAL,)),
     ]
     anywhere = pl.BlockSpec(memory_space=pl.ANY)
@@ -434,14 +437,44 @@
     )(lengths, *(pltpu.with_memory_space_constraint(a, pltpu.HBM) for a in (inp, cot, frz, adn, aup)))
 
 
+def close(lengths, raw, gd, gu, og_out, gd_out, gu_out, masked, sem):
+    copies = [
+        pltpu.make_async_copy(gd, gd_out, sem.at[0]),
+        pltpu.make_async_copy(gu, gu_out, sem.at[1]),
+    ]
+    rows = raw.shape[0]
+    n = masked.shape[1]
+    for i in range(rows // n):
+        at = pl.ds(i * n, n)
+        position = lax.axis_index("ctx") * rows + i * n
+        position = position + lax.broadcasted_iota(jnp.int32, (n, 1), 0)
+        masked[i] = jnp.where(position < lengths[0], raw[at, :], jnp.zeros((), BF16))
+        copies.append(pltpu.make_async_copy(masked.at[i], og_out.at[at], sem.at[2 + i]))
+        copies[-1].start()
+        if i == 0:
+            for copy in copies[:2]:
+                copy.start()
+    for copy in copies:
+        copy.wait()
+
+
 def shard(inputs, cotangent, lengths, frozen, adapter_down, adapter_up):
     _, rows, features = inputs.shape
-    raw, grad_down, grad_up = fused(
-        lengths, inputs[0], cotangent[0], frozen, adapter_down, adapter_up
-    )
-    position = lax.axis_index("ctx") * rows + jnp.arange(rows, dtype=jnp.int32)
-    live = position[:, None] < lengths
-    input_grads = jnp.where(live, raw, jnp.zeros((), BF16))
+    results = fused(lengths, inputs[0], cotangent[0], frozen, adapter_down, adapter_up)
+    vmem = pl.BlockSpec(memory_space=pltpu.VMEM)
+    hbm = pl.BlockSpec(memory_space=pltpu.HBM)
+    n = 16
+    input_grads, grad_down, grad_up = pl.pallas_call(
+        close,
+        out_shape=[jax.ShapeDtypeStruct(r.shape, r.dtype) for r in results],
+        in_specs=[pl.BlockSpec(memory_space=pltpu.SMEM)] + [vmem] * 3,
+        out_specs=[hbm] * 3,
+        scratch_shapes=[
+            pltpu.VMEM((rows // n, n, features), BF16),
+            pltpu.SemaphoreType.DMA((2 + rows // n,)),
+        ],
+        compiler_params=pltpu.CompilerParams(vmem_limit_bytes=16 << 20),
+    )(lengths, *results)
     return input_grads[None], grad_down, grad_up
 
 

time: 90.2 us -> 87.7 us (0.972)
  other arithmetic: 2.36 us -> 0 us
  local copies, waits for them, and re-layouts: 1.62 us -> 0 us
  Pallas kernels: 84.9 us -> 86.3 us
    pallas_call x0 -> x1, Pallas kernels: none -> 2.51 us  [shard(): pl.pallas_call(close, out_shape=[jax.ShapeDtypeStruct(r.shape, r.dtype) f...]
    broadcast_in_dim x1 -> x0, other arithmetic: 2.36 us -> none  [shard(): return (input_grads[None], grad_down, grad_up)]
    unnamed x2 -> x0, local copies, waits for them, and re-layouts: 1.62 us -> none
    pallas_call x1, Pallas kernels: 84.9 us -> 83.8 us  [fused(): pl.pallas_call(body, out_shape=(jax.ShapeDtypeStruct((rows, features), BF...]
where the time goes in v4:
time: 87.7 us; the launch traced here: 87.6 us
  Pallas kernels  86.3 us (98%)
  between operations  1.29 us (1%)
    pallas_call x1, Pallas kernels, fused(): pl.pallas_call(body, out_shape=(jax.ShapeDtypeStruct((rows, features), BF...  83.8 us
    pallas_call x1, Pallas kernels, shard(): pl.pallas_call(close, out_shape=[jax.ShapeDtypeStruct(r.shape, r.dtype) f...  2.51 us

profile of v4, /device:TPU:1, one launch (start us, length us, event | category | flops | bytes accessed | tf_op | source)
XLA Modules:
  0.0 87.6 jit_solution(2751254348483314321)
XLA Ops:
  1.3 83.8 %shard_map.85 = (bf16[128,16384]{1,0:T(8,128)(2,1)S(1)}, f32[16,16384]{1,0:T(8,128)S(1)}, f32[16,2048]{1,0:T(8,128)S(1)}) custom-call(s32[1]{0:T(128)S(6)} %copy.9.lengths, bf16[128,16384]{1,0:T(8,128)(2,1)} %bitcast.3, bf16[128,2048]{1,0:T(8,128)(2,1)} %bitcast.4, bf16[128,2048]{1,0:T(8,128)(2,1)} %frz.1, bf16[16,16384]{1,0:T(8,128)(2,1)} %adn.1, ...), custom_call_target="tpu_custom_call" | custom-call | tf_op jit(solution)/shard_map/pallas_call | solution.py:424
  85.1 2.5 %shard_map.86 = (bf16[128,16384]{1,0:T(8,128)(2,1)}, f32[16,16384]{1,0:T(8,128)}, f32[16,2048]{1,0:T(8,128)}) custom-call(s32[1]{0:T(128)S(6)} %copy.9.lengths, bf16[128,16384]{1,0:T(8,128)(2,1)S(1)} %get-tuple-element.9.raw, f32[16,16384]{1,0:T(8,128)S(1)} %get-tuple-element.10.gd, f32[16,2048]{1,0:T(8,128)S(1)} %get-tuple-element.11.gu), custom_call_target="tpu_custom_call" | custom-call | tf_op jit(solution)/shard_map/pallas_call | solution.py:467

commit v5 on v4

--- a/solution.py
+++ b/solution.py
@@ -51,10 +51,8 @@
         ll = 1 - lo if flip_lo else lo
         return (ll, zz * 2 + cc, xx * 2 + hh)
 
-    peers = [dict(dx=dx, dc=dc) for dx in range(X) for dc in range(2) if dx or dc]
-    peers += [dict(dz=dz) for dz in range(1, Z)]
-    peers += [dict(dx=dx, flip_hi=1) for dx in range(X)]
-    peers += [dict(flip_hi=1, flip_lo=1), dict(flip_lo=1)]
+    peers = [dict(dx=1), dict(dx=-1), dict(dz=1), dict(dz=-1), dict(dc=1)]
+    peers += [dict(flip_hi=1), dict(flip_lo=1), dict(flip_hi=1, flip_lo=1)]
 
     def send(src, dst, name, i, **to):
         r = BASE[name] + min(i, SEMS[name] - 1)

time: 87.7 us -> 86.3 us (0.984)
  Pallas kernels: 86.3 us -> 84.9 us
    pallas_call x1, Pallas kernels: 83.8 us -> 82.4 us  [fused(): pl.pallas_call(body, out_shape=(jax.ShapeDtypeStruct((rows, features), BF...]
where the time goes in v5:
time: 86.3 us; the launch traced here: 86.2 us
  Pallas kernels  84.9 us (98%)
  between operations  1.29 us (1%)
    pallas_call x1, Pallas kernels, fused(): pl.pallas_call(body, out_shape=(jax.ShapeDtypeStruct((rows, features), BF...  82.4 us
    pallas_call x1, Pallas kernels, shard(): pl.pallas_call(close, out_shape=[jax.ShapeDtypeStruct(r.shape, r.dtype) f...  2.51 us

profile of v5, /device:TPU:1, one launch (start us, length us, event | category | flops | bytes accessed | tf_op | source)
XLA Modules:
  0.0 86.2 jit_solution(16916246797787616748)
XLA Ops:
  1.3 82.4 %shard_map.85 = (bf16[128,16384]{1,0:T(8,128)(2,1)S(1)}, f32[16,16384]{1,0:T(8,128)S(1)}, f32[16,2048]{1,0:T(8,128)S(1)}) custom-call(s32[1]{0:T(128)S(6)} %copy.9.lengths, bf16[128,16384]{1,0:T(8,128)(2,1)} %bitcast.3, bf16[128,2048]{1,0:T(8,128)(2,1)} %bitcast.4, bf16[128,2048]{1,0:T(8,128)(2,1)} %frz.1, bf16[16,16384]{1,0:T(8,128)(2,1)} %adn.1, ...), custom_call_target="tpu_custom_call" | custom-call | tf_op jit(solution)/shard_map/pallas_call | solution.py:422
  83.7 2.5 %shard_map.86 = (bf16[128,16384]{1,0:T(8,128)(2,1)}, f32[16,16384]{1,0:T(8,128)}, f32[16,2048]{1,0:T(8,128)}) custom-call(s32[1]{0:T(128)S(6)} %copy.9.lengths, bf16[128,16384]{1,0:T(8,128)(2,1)S(1)} %get-tuple-element.9.raw, f32[16,16384]{1,0:T(8,128)S(1)} %get-tuple-element.10.gd, f32[16,2048]{1,0:T(8,128)S(1)} %get-tuple-element.11.gu), custom_call_target="tpu_custom_call" | custom-call | tf_op jit(solution)/shard_map/pallas_call | solution.py:465

commit v6 on v5

--- a/solution.py
+++ b/solution.py
@@ -184,20 +184,21 @@
         total = g8[z]
         for dz in range(1, Z):
             total = total + r5[dz - 1]
-        c7[z] = total * (1.0 / 32.0)
+        c7[x] = total * (1.0 / 32.0)
+        for dx in range(1, X):
+            send(c7.at[x], c7.at[x], "s8", dx - 1, dx=dx)
+
+    def stage8():
+        got(c7.at[pl.ds(0, 3)], "s8")
+        c8[z] = c7[...]
         for dz in range(1, Z):
-            send(c7.at[z], c7.at[z], "s7", dz - 1, dz=dz)
-
-    def stage8():
-        got(c7.at[pl.ds(0, 7)], "s7")
-        c8[x] = c7[:6]
-        for dx in range(1, X):
-            send(c7.at[pl.ds(0, 6)], c8.at[x], "s8", dx - 1, dx=dx)
+            send(c7, c8.at[z], "s7", dz - 1, dz=dz)
 
     def stage9():
-        got(c8.at[pl.ds(0, 3)], "s8")
-        c9[hi] = c8[...]
-        send(c8, c9.at[hi], "s9", 0, flip_hi=1, flip_lo=1)
+        got(c8.at[pl.ds(0, 7)], "s7")
+        six = c8.at[pl.ds(0, 6)]
+        c9[hi] = six[...]
+        send(six, c9.at[hi], "s9", 0, flip_hi=1, flip_lo=1)
 
     def stage10():
         got(c9.at[1 - hi], "s9", 0)
@@ -212,7 +213,7 @@
             for cc in range(2):
                 for o in range(6):
                     r = slice((o % 2) * 8, (o % 2) * 8 + 8)
-                    v = c10[cc, j % 2, j // 2, o]
+                    v = c10[cc, j % 2, o, j // 2]
                     at = cc * 3 * n + (o // 2) * n
                     k = max(0, min(n, dcol - at))
                     if k:
@@ -354,8 +355,8 @@
     weights(7)
     across(6)
     product(5)
+    across(7)
     stage8()
-    across(7)
     product(6)
     across(8)
     product(7)
@@ -377,9 +378,9 @@
     left(r4, "s4")
     left(r5, "s5")
     left(r6, "s6")
-    left(c7.at[pl.ds(0, 7)], "s7")
-    left(c8.at[pl.ds(0, 3)], "s8")
-    left(c8, "s9")
+    left(c8.at[pl.ds(0, 7)], "s7")
+    left(c7.at[pl.ds(0, 3)], "s8")
+    left(c8.at[pl.ds(0, 6)], "s9")
     left(c9, "s10")
 
 
@@ -408,10 +409,10 @@
         pltpu.VMEM((rank, share // 2), F32),
         pltpu.VMEM((Z, 8, n), F32),
         pltpu.VMEM((Z - 1, 8, n), F32),
-        pltpu.VMEM((Z, 8, n), F32),
-        pltpu.VMEM((X, 6, 8, n), F32),
-        pltpu.VMEM((2, X, 6, 8, n), F32),
-        pltpu.VMEM((2, 2, X, 6, 8, n), F32),
+        pltpu.VMEM((X, 8, n), F32),
+        pltpu.VMEM((Z, X, 8, n), F32),
+        pltpu.VMEM((2, 6, X, 8, n), F32),
+        pltpu.VMEM((2, 2, 6, X, 8, n), F32),
         pltpu.VMEM((rank, features), F32),
         pltpu.VMEM((rank, width), F32),
         pltpu.SemaphoreType.DMA((13,)),

time: 86.3 us -> 84.3 us (0.977)
  Pallas kernels: 84.9 us -> 82.9 us
    pallas_call x1, Pallas kernels: 82.4 us -> 80.4 us  [fused(): pl.pallas_call(body, out_shape=(jax.ShapeDtypeStruct((rows, features), BF...]
where the time goes in v6:
time: 84.3 us; the launch traced here: 84.2 us
  Pallas kernels  82.9 us (98%)
  between operations  1.29 us (2%)
    pallas_call x1, Pallas kernels, fused(): pl.pallas_call(body, out_shape=(jax.ShapeDtypeStruct((rows, features), BF...  80.4 us
    pallas_call x1, Pallas kernels, shard(): pl.pallas_call(close, out_shape=[jax.ShapeDtypeStruct(r.shape, r.dtype) f...  2.51 us

profile of v6, /device:TPU:1, one launch (start us, length us, event | category | flops | bytes accessed | tf_op | source)
XLA Modules:
  0.0 84.2 jit_solution(12131449544831692799)
XLA Ops:
  1.3 80.4 %shard_map.85 = (bf16[128,16384]{1,0:T(8,128)(2,1)S(1)}, f32[16,16384]{1,0:T(8,128)S(1)}, f32[16,2048]{1,0:T(8,128)S(1)}) custom-call(s32[1]{0:T(128)S(6)} %copy.9.lengths, bf16[128,16384]{1,0:T(8,128)(2,1)} %bitcast.3, bf16[128,2048]{1,0:T(8,128)(2,1)} %bitcast.4, bf16[128,2048]{1,0:T(8,128)(2,1)} %frz.1, bf16[16,16384]{1,0:T(8,128)(2,1)} %adn.1, ...), custom_call_target="tpu_custom_call" | custom-call | tf_op jit(solution)/shard_map/pallas_call | solution.py:423
  81.7 2.5 %shard_map.86 = (bf16[128,16384]{1,0:T(8,128)(2,1)}, f32[16,16384]{1,0:T(8,128)}, f32[16,2048]{1,0:T(8,128)}) custom-call(s32[1]{0:T(128)S(6)} %copy.9.lengths, bf16[128,16384]{1,0:T(8,128)(2,1)S(1)} %get-tuple-element.9.raw, f32[16,16384]{1,0:T(8,128)S(1)} %get-tuple-element.10.gd, f32[16,2048]{1,0:T(8,128)S(1)} %get-tuple-element.11.gu), custom_call_target="tpu_custom_call" | custom-call | tf_op jit(solution)/shard_map/pallas_call | solution.py:466
